TPU v7x, 256 devices: a whole 4x4x8 slice. The times are simulated.
256 devices in a mesh: row: 16 (over x, y), col: 8 (over z_lo, core), layer: 2 (over z_hi).
Axes of the slice: x: 4, y: 4, z: 8 (z_hi: 2, z_lo: 4; z = z_hi * 4 + z_lo), core: 2. Of those that a mesh axis runs over, the one named last changes fastest.
Arguments:
- tasks: bfloat16 [16384, 4096], P(('row', 'col')), may hold values from -0.1875 to 0.1875
- task_owner: int32 [16384, 1], P(('row', 'col')), may hold values from 0 to 127; in each aligned block of 128 rows (0 to 127, 128 to 255, ...) at most 2 rows name the same one
- task_slot: int32 [16384], P(('row', 'col')), may hold values from 0 to 127
- p_pattern: int32 [128, 128], P('row', 'col'), may hold values from 0 to 1, as said below
- c_pattern: int32 [128, 128], P('row', 'col'), may hold values from 0 to 1, as said below
- occupations: float32 [8192], P('row'), may hold values from 0.1 to 0.9
Outputs:
- purified: float32 [8192, 8192], P(('row', 'layer'), 'col')
Inputs may be any that keep to these rules, and one draw needn't show every extreme that they name: `task_owner`: the 128 tasks of one index of row and col name each owner at most 2 times. `task_slot`: a block of the owner's 8 x 16 blocks, row-major. `p_pattern`: 0 or 1; every diagonal block is 1. `c_pattern`: 0 or 1; every diagonal block is 1.
All inputs are finite; a program needn't handle non-finite values.
Results may differ from a plain program's by a relative error of at most 0.025.
Values may be sent and summed in bfloat16 or wider, within the bound.
A program may use at most 64 MiB of HBM per device.

v0:
```python
import jax
import jax.numpy as jnp
from jax import lax
from jax.sharding import PartitionSpec as P

BLK = 64


def expand_blocks(pattern):
    return jnp.repeat(jnp.repeat(pattern.astype(jnp.float32), BLK, axis=0), BLK, axis=1)


def column_units(tile, layers, layer):
    rows, cols = tile.shape
    unit = rows // layers
    split = tile.reshape(rows, cols // (layers * unit), layers, unit)
    picked = lax.dynamic_index_in_dim(split, layer, axis=2, keepdims=False)
    return picked.reshape(rows, cols // layers)


def row_unit(tile, layers, layer):
    unit = tile.shape[0] // layers
    return lax.dynamic_slice_in_dim(tile, layer * unit, unit, 0)


def fold_rows(piece_rows, left_panel):
    return jnp.dot(
        left_panel,
        lax.all_gather(piece_rows, "row", axis=0, tiled=True),
        preferred_element_type=jnp.float32,
    )


def on_device(tasks, task_owner, task_slot, p_pattern, c_pattern, occupations):
    owners = lax.axis_size("row") * lax.axis_size("col")
    task_count = tasks.shape[0]
    capacity = max(2, 2 * task_count // owners)
    block_rows, block_cols = p_pattern.shape
    slots_here = block_rows * block_cols
    owner = task_owner[:, 0]
    same = (owner[:, None] == jnp.arange(owners, dtype=jnp.int32)[None, :]).astype(jnp.int32)
    placed = jnp.sum(jnp.cumsum(same, axis=0) * same, axis=1) - 1
    target = owner * capacity + placed
    send_blocks = jnp.zeros((owners * capacity, BLK * BLK), jnp.bfloat16).at[target].set(tasks)
    send_slots = (
        jnp.full((owners * capacity,), -1.0, jnp.bfloat16)
        .at[target]
        .set(task_slot.astype(jnp.bfloat16))
    )
    got_blocks, got_slots = (
        lax.all_to_all(
            send_blocks.reshape(owners, capacity, BLK * BLK),
            ("row", "col"),
            split_axis=0,
            concat_axis=0,
            tiled=True,
        ),
        lax.all_to_all(
            send_slots.reshape(owners, capacity),
            ("row", "col"),
            split_axis=0,
            concat_axis=0,
            tiled=True,
        ),
    )
    marks = (
        got_slots.reshape(-1).astype(jnp.float32)[:, None]
        == jnp.arange(slots_here, dtype=jnp.float32)[None, :]
    ).astype(jnp.bfloat16)
    summed = lax.dot_general(
        marks,
        got_blocks.reshape(-1, BLK * BLK),
        (((0,), (0,)), ((), ())),
        preferred_element_type=jnp.float32,
    )
    tile_rows = block_rows * BLK
    tile_cols = block_cols * BLK
    assembled = (
        summed.reshape(block_rows, block_cols, BLK, BLK)
        .transpose(0, 2, 1, 3)
        .reshape(tile_rows, tile_cols)
    )
    row_start = lax.axis_index("row") * tile_rows
    col_start = lax.axis_index("col") * tile_cols
    on_diagonal = (row_start + jnp.arange(tile_rows))[:, None] == (
        col_start + jnp.arange(tile_cols)
    )[None, :]
    density = (
        expand_blocks(p_pattern) * assembled + jnp.where(on_diagonal, occupations[:, None], 0.0)
    ).astype(jnp.bfloat16)
    layers = lax.axis_size("layer")
    layer = lax.axis_index("layer")
    left_piece = column_units(density, layers, layer)
    right_piece = row_unit(density, layers, layer)
    left_panel = lax.all_gather(left_piece, "col", axis=1, tiled=True)
    partial_square = fold_rows(right_piece, left_panel)
    square = lax.psum(partial_square.astype(jnp.bfloat16), "layer").astype(jnp.float32)
    square_rows = row_unit(square, layers, layer)
    partial_cube = fold_rows(square_rows.astype(jnp.bfloat16), left_panel)
    cube_rows = row_unit(
        lax.psum(partial_cube.astype(jnp.bfloat16), "layer").astype(jnp.float32), layers, layer
    )
    mask_rows = row_unit(expand_blocks(c_pattern), layers, layer)
    return mask_rows * (3.0 * square_rows - 2.0 * cube_rows)


def solution(mesh):
    return jax.shard_map(
        on_device,
        mesh=mesh,
        in_specs=(
            P(("row", "col"), None),
            P(("row", "col"), None),
            P(("row", "col")),
            P("row", "col"),
            P("row", "col"),
            P("row"),
        ),
        out_specs=P(("row", "layer"), "col"),
        check_vma=False,
    )
```

profile of v0, /device:TPU:1, one launch (start us, length us, event | category | flops | bytes accessed | tf_op | source)
XLA Modules:
  0.0 508.8 jit_solution(2555189373644705348)
XLA Ops:
  6.5 0.7 convert_element_type.47
  7.2 0.7 fusion.12
  8.1 0.8 select_reduce_fusion
  8.9 0.7 fusion.13
  9.6 1.3 scatter_custom_fusion
  11.0 0.8 all_to_all.12
  11.8 13.8 %all-to-all-start = ((bf16[128,1,2]{2,1,0:T(2,128)(2,1)}), bf16[128,1,2]{2,1,0:T(2,128)(2,1)S(1)}, u32[]{:S(2)}, u32[]{:S(2)}) async-start(bf16[128,1,2]{2,1,0:T(2,128)(2,1)} %all_to_all.12), calls=%async_computation | async-start | bytes 131072 | tf_op jit(solution)/shard_map/all_to_all | solution.py:58
  25.6 3.4 scatter_custom_fusion.1
  29.0 2.6 reshape.102
  31.6 3.6 all-to-all-done
  35.3 8.2 %all-to-all-start.1 = ((bf16[128,2,4096]{2,1,0:T(2,128)(2,1)}), bf16[128,2,4096]{2,1,0:T(2,128)(2,1)S(1)}, u32[]{:S(2)}, u32[]{:S(2)}) async-start(bf16[128,2,4096]{2,1,0:T(2,128)(2,1)} %reshape.102), calls=%async_computation.1 | async-start | bytes 4194304 | tf_op jit(solution)/shard_map/all_to_all | solution.py:51
  44.4 51.1 %all-to-all-done.1 = bf16[128,2,4096]{2,1,0:T(2,128)(2,1)S(1)} async-done(((bf16[128,2,4096]{2,1,0:T(2,128)(2,1)}), bf16[128,2,4096]{2,1,0:T(2,128)(2,1)S(1)}, u32[]{:S(2)}, u32[]{:S(2)}) %all-to-all-start.1) | async-done | bytes 2097184 | tf_op jit(solution)/shard_map/all_to_all | solution.py:51
  95.5 2.2 reshape.103
  97.7 3.3 copy.17
  101.0 3.2 convolution_bitcast_fusion
  104.2 4.1 reshape.104
  108.3 1.9 constant_dynamic-slice_fusion.2
  110.2 2.4 copy.22
  112.8 1.0 fusion.5
  114.0 4.9 reshape.107
  118.9 2.3 constant_dynamic-slice_fusion.1
  121.2 1.6 copy.23
  122.8 1.0 fusion.3
  123.9 38.4 %all-gather.4.cloned.1.call-done = bf16[512,4096]{0,1:T(8,128)(2,1)} async-done(((bf16[512,512]{0,1:T(8,128)(2,1)}), bf16[512,4096]{0,1:T(8,128)(2,1)}) %all-gather.4.cloned.1.call-update) | async-done | bytes 4194320 | tf_op jit(solution)/shard_map/all_gather | solution.py:95
  162.3 85.9 %all-gather.6.cloned.1.call-done = bf16[4096,1024]{0,1:T(8,128)(2,1)} async-done(((bf16[256,1024]{0,1:T(8,128)(2,1)}), bf16[4096,1024]{0,1:T(8,128)(2,1)}) %all-gather.6.cloned.1.call-update) | async-done | bytes 8388624 | tf_op jit(solution)/shard_map/all_gather | solution.py:29
  248.2 10.2 %convolution_convert_fusion.1 = bf16[512,1024]{1,0:T(8,128)(2,1)} fusion(bf16[512,4096]{0,1:T(8,128)(2,1)} %all-gather.4.cloned.1.call-done, bf16[4096,1024]{0,1:T(8,128)(2,1)} %all-gather.6.cloned.1.call-done), kind=kOutput, calls=%fused_computation.4 | convolution fusion | flops 4295491584 | bytes 13631488 | tf_op jit(solution)/shard_map/dot_general | solution.py:27
  258.5 78.6 %all-reduce.3.cloned.1.call-done = bf16[512,1024]{1,0:T(8,128)(2,1)} async-done(((bf16[512,1024]{1,0:T(8,128)(2,1)}), bf16[512,1024]{1,0:T(8,128)(2,1)}) %all-reduce.3.cloned.1.call-update) | async-done | bytes 1048592 | tf_op jit(solution)/shard_map/psum | solution.py:97
  337.1 1.9 convert_convert_fusion
  339.3 72.5 %all-gather.8.cloned.1.call-done = bf16[4096,1024]{1,0:T(8,128)(2,1)} async-done(((bf16[256,1024]{1,0:T(8,128)(2,1)}), bf16[4096,1024]{1,0:T(8,128)(2,1)}) %all-gather.8.cloned.1.call-update) | async-done | bytes 8388624 | tf_op jit(solution)/shard_map/all_gather | solution.py:29
  411.8 10.1 %convolution_convert_fusion = bf16[512,1024]{1,0:T(8,128)(2,1)} fusion(bf16[512,4096]{0,1:T(8,128)(2,1)} %all-gather.4.cloned.1.call-done, bf16[4096,1024]{1,0:T(8,128)(2,1)} %all-gather.8.cloned.1.call-done), kind=kOutput, calls=%fused_computation.3 | convolution fusion | flops 4295491584 | bytes 13631488 | tf_op jit(solution)/shard_map/dot_general | solution.py:27
  422.9 77.1 %all-reduce.5.cloned.1.call-done = bf16[512,1024]{1,0:T(8,128)(2,1)} async-done(((bf16[512,1024]{1,0:T(8,128)(2,1)}), bf16[512,1024]{1,0:T(8,128)(2,1)}) %all-reduce.5.cloned.1.call-update) | async-done | bytes 1048592 | tf_op jit(solution)/shard_map/psum | solution.py:101
  500.0 2.2 fusion.1
  (40 shorter events, 2.8 us)
Async XLA Ops:
  11.8 23.5 %all-to-all-start = ((bf16[128,1,2]{2,1,0:T(2,128)(2,1)}), bf16[128,1,2]{2,1,0:T(2,128)(2,1)S(1)}, u32[]{:S(2)}, u32[]{:S(2)}) async-start(bf16[128,1,2]{2,1,0:T(2,128)(2,1)} %all_to_all.12), calls=%async_computation | async-start | bytes 131072 | tf_op jit(solution)/shard_map/all_to_all | solution.py:58
  31.6 12.1 %copy-start.2 = (s32[8,16]{1,0:T(8,128)S(1)}, s32[8,16]{1,0:T(8,128)}, u32[]{:S(2)}) copy-start(s32[8,16]{1,0:T(8,128)} %param.9) | copy-start | bytes 1540
  35.3 60.2 %all-to-all-start.1 = ((bf16[128,2,4096]{2,1,0:T(2,128)(2,1)}), bf16[128,2,4096]{2,1,0:T(2,128)(2,1)S(1)}, u32[]{:S(2)}, u32[]{:S(2)}) async-start(bf16[128,2,4096]{2,1,0:T(2,128)(2,1)} %reshape.102), calls=%async_computation.1 | async-start | bytes 4194304 | tf_op jit(solution)/shard_map/all_to_all | solution.py:51
  43.5 118.8 %all-gather.4.cloned.1.call-start = ((), (), s32[]{:S(2)}) async-start(), calls=%async_computation.2 | async-start | bytes 4718592 | tf_op jit(solution)/shard_map/all_gather | solution.py:95
  110.2 2.6 copy-start.1
  113.8 134.4 %all-gather.6.cloned.1.call-start = ((), (), s32[]{:S(2)}) async-start(), calls=%async_computation.3 | async-start | bytes 8912896 | tf_op jit(solution)/shard_map/all_gather | solution.py:29
  123.8 213.3 %all-reduce.3.cloned.1.call-start = ((), (), s32[]{:S(2)}) async-start(), calls=%async_computation.4 | async-start | bytes 2097152 | tf_op jit(solution)/shard_map/psum | solution.py:97
  258.4 153.4 %all-gather.8.cloned.1.call-start = ((), (), s32[]{:S(2)}) async-start(), calls=%async_computation.5 | async-start | bytes 8912896 | tf_op jit(solution)/shard_map/all_gather | solution.py:29
  339.0 82.9 %copy-start.3 = (s32[8,16]{1,0:T(8,128)S(1)}, s32[8,16]{1,0:T(8,128)}, u32[]{:S(2)}) copy-start(s32[8,16]{1,0:T(8,128)} %param.10) | copy-start | bytes 1540
  339.0 161.0 %all-reduce.5.cloned.1.call-start = ((), (), s32[]{:S(2)}) async-start(), calls=%async_computation.6 | async-start | bytes 2097152 | tf_op jit(solution)/shard_map/psum | solution.py:101
  422.5 77.6 %copy-start = (bf16[512,1024]{1,0:T(8,128)(2,1)S(1)}, bf16[512,1024]{1,0:T(8,128)(2,1)}, u32[]{:S(2)}) copy-start(bf16[512,1024]{1,0:T(8,128)(2,1)} %all-reduce.3.cloned.1.call-done) | copy-start | bytes 3145732
Sparse Core Ops, SparseCore 0:
  114.0 48.3 all-gather.3
  164.7 83.4 all-gather.5
  258.5 78.5 all-reduce.2
  339.7 72.0 all-gather.7
  422.1 77.9 all-reduce.4
where the time goes:
time: 510 us; the launch traced here: 509 us
  waiting for transfers between devices  407 us (80%)
  local copies, waits for them, and re-layouts  32.5 us (6%)
  matrix products  23.5 us (5%)
  starting transfers between devices  22.7 us (4%)
  between operations  13.4 us (3%)
  other arithmetic  9.42 us (2%)
    all_gather x2, waiting for transfers between devices, fold_rows(): lax.all_gather(piece_rows, 'row', axis=0, tiled=True)  158 us
    psum x1, waiting for transfers between devices, on_device(): lax.psum(partial_square.astype(jnp.bfloat16), 'layer').astype(jnp.float32)  78.6 us
    psum x1, waiting for transfers between devices, on_device(): lax.psum(partial_cube.astype(jnp.bfloat16), 'layer').astype(jnp.float32)  77.1 us
    all_to_all x1, waiting for transfers between devices, on_device(): lax.all_to_all(send_blocks.reshape(owners, capacity, BLK * BLK), ('row',...  51.1 us
    all_gather x1, waiting for transfers between devices, on_device(): left_panel = lax.all_gather(left_piece, 'col', axis=1, tiled=True)  38.4 us
    dot_general x2, matrix products, fold_rows(): jnp.dot(left_panel, lax.all_gather(piece_rows, 'row', axis=0, tiled=True)...  20.3 us
    all_to_all x1, starting transfers between devices, on_device(): lax.all_to_all(send_slots.reshape(owners, capacity), ('row', 'col'), spli...  13.8 us
  transfers between devices with their start and end apart: 7, of which 7 were waited for; matrix products, arithmetic and copies ran while one was open for 3% of the time, Pallas kernels for 0%

commit v1 on v0

--- a/solution.py
+++ b/solution.py
@@ -98,7 +98,11 @@
     square_rows = row_unit(square, layers, layer)
     partial_cube = fold_rows(square_rows.astype(jnp.bfloat16), left_panel)
     cube_rows = row_unit(
-        lax.psum(partial_cube.astype(jnp.bfloat16), "layer").astype(jnp.float32), layers, layer
+        jnp.sum(lax.all_gather(partial_cube.astype(jnp.bfloat16), "layer"), axis=0).astype(
+            jnp.float32
+        ),
+        layers,
+        layer,
     )
     mask_rows = row_unit(expand_blocks(c_pattern), layers, layer)
     return mask_rows * (3.0 * square_rows - 2.0 * cube_rows)

time: 510 us -> 498 us (0.976)
  waiting for transfers between devices: 407 us -> 394 us
    psum x1 -> x0, waiting for transfers between devices: 77.1 us -> none  [on_device(): lax.psum(partial_cube.astype(jnp.bfloat16), 'layer').astype(jnp.float32)]
    all_gather x0 -> x1, waiting for transfers between devices: none -> 64.1 us  [on_device(): lax.all_gather(partial_cube.astype(jnp.bfloat16), 'layer')]
  transfers between devices with their start and end apart: 7 -> 7, of which waited for: 7 -> 7; matrix products, arithmetic and copies ran while one was open for 3% -> 4% of each run, Pallas kernels for 0% -> 0%
where the time goes in v1:
time: 498 us; the launch traced here: 497 us
  waiting for transfers between devices  394 us (79%)
  local copies, waits for them, and re-layouts  32.5 us (7%)
  matrix products  23.5 us (5%)
  starting transfers between devices  22.7 us (5%)
  between operations  13.4 us (3%)
  other arithmetic  10.5 us (2%)
    all_gather x2, waiting for transfers between devices, fold_rows(): lax.all_gather(piece_rows, 'row', axis=0, tiled=True)  158 us
    psum x1, waiting for transfers between devices, on_device(): lax.psum(partial_square.astype(jnp.bfloat16), 'layer').astype(jnp.float32)  78.6 us
    all_gather x1, waiting for transfers between devices, on_device(): lax.all_gather(partial_cube.astype(jnp.bfloat16), 'layer')  64.1 us
    all_to_all x1, waiting for transfers between devices, on_device(): lax.all_to_all(send_blocks.reshape(owners, capacity, BLK * BLK), ('row',...  51.1 us
    all_gather x1, waiting for transfers between devices, on_device(): left_panel = lax.all_gather(left_piece, 'col', axis=1, tiled=True)  38.4 us
    dot_general x2, matrix products, fold_rows(): jnp.dot(left_panel, lax.all_gather(piece_rows, 'row', axis=0, tiled=True)...  20.3 us
    all_to_all x1, starting transfers between devices, on_device(): lax.all_to_all(send_slots.reshape(owners, capacity), ('row', 'col'), spli...  13.8 us
  transfers between devices with their start and end apart: 7, of which 7 were waited for; matrix products, arithmetic and copies ran while one was open for 4% of the time, Pallas kernels for 0%

profile of v1, /device:TPU:1, one launch (start us, length us, event | category | flops | bytes accessed | tf_op | source)
XLA Modules:
  0.0 496.9 jit_solution(7564973283632156204)
XLA Ops:
  7.2 0.7 fusion.12
  8.1 0.8 select_reduce_fusion
  8.9 0.7 fusion.13
  9.6 1.3 scatter_custom_fusion
  11.0 0.8 all_to_all.12
  11.8 13.8 %all-to-all-start = ((bf16[128,1,2]{2,1,0:T(2,128)(2,1)}), bf16[128,1,2]{2,1,0:T(2,128)(2,1)S(1)}, u32[]{:S(2)}, u32[]{:S(2)}) async-start(bf16[128,1,2]{2,1,0:T(2,128)(2,1)} %all_to_all.12), calls=%async_computation | async-start | bytes 131072 | tf_op jit(solution)/shard_map/all_to_all | solution.py:58
  25.6 3.4 scatter_custom_fusion.1
  29.0 2.6 reshape.102
  31.6 3.6 all-to-all-done
  35.3 8.2 %all-to-all-start.1 = ((bf16[128,2,4096]{2,1,0:T(2,128)(2,1)}), bf16[128,2,4096]{2,1,0:T(2,128)(2,1)S(1)}, u32[]{:S(2)}, u32[]{:S(2)}) async-start(bf16[128,2,4096]{2,1,0:T(2,128)(2,1)} %reshape.102), calls=%async_computation.1 | async-start | bytes 4194304 | tf_op jit(solution)/shard_map/all_to_all | solution.py:51
  44.4 51.1 %all-to-all-done.1 = bf16[128,2,4096]{2,1,0:T(2,128)(2,1)S(1)} async-done(((bf16[128,2,4096]{2,1,0:T(2,128)(2,1)}), bf16[128,2,4096]{2,1,0:T(2,128)(2,1)S(1)}, u32[]{:S(2)}, u32[]{:S(2)}) %all-to-all-start.1) | async-done | bytes 2097184 | tf_op jit(solution)/shard_map/all_to_all | solution.py:51
  95.5 2.2 reshape.103
  97.7 3.3 copy.17
  101.0 3.2 convolution_bitcast_fusion
  104.2 4.1 reshape.104
  108.3 1.9 constant_dynamic-slice_fusion.2
  110.2 2.4 copy.22
  112.8 1.0 fusion.5
  114.0 4.9 reshape.107
  118.9 2.3 constant_dynamic-slice_fusion.1
  121.2 1.6 copy.23
  122.8 1.0 fusion.3
  123.9 38.4 %all-gather.6.cloned.1.call-done = bf16[512,4096]{0,1:T(8,128)(2,1)} async-done(((bf16[512,512]{0,1:T(8,128)(2,1)}), bf16[512,4096]{0,1:T(8,128)(2,1)}) %all-gather.6.cloned.1.call-update) | async-done | bytes 4194320 | tf_op jit(solution)/shard_map/all_gather | solution.py:95
  162.3 85.9 %all-gather.8.cloned.1.call-done = bf16[4096,1024]{0,1:T(8,128)(2,1)} async-done(((bf16[256,1024]{0,1:T(8,128)(2,1)}), bf16[4096,1024]{0,1:T(8,128)(2,1)}) %all-gather.8.cloned.1.call-update) | async-done | bytes 8388624 | tf_op jit(solution)/shard_map/all_gather | solution.py:29
  248.2 10.2 %convolution_convert_fusion.1 = bf16[512,1024]{1,0:T(8,128)(2,1)} fusion(bf16[512,4096]{0,1:T(8,128)(2,1)} %all-gather.6.cloned.1.call-done, bf16[4096,1024]{0,1:T(8,128)(2,1)} %all-gather.8.cloned.1.call-done), kind=kOutput, calls=%fused_computation.4 | convolution fusion | flops 4295491584 | bytes 13631488 | tf_op jit(solution)/shard_map/dot_general | solution.py:27
  258.5 78.6 %all-reduce.2.cloned.1.call-done = bf16[512,1024]{1,0:T(8,128)(2,1)} async-done(((bf16[512,1024]{1,0:T(8,128)(2,1)}), bf16[512,1024]{1,0:T(8,128)(2,1)}) %all-reduce.2.cloned.1.call-update) | async-done | bytes 1048592 | tf_op jit(solution)/shard_map/psum | solution.py:97
  337.1 1.9 convert_convert_fusion
  339.3 72.5 %all-gather.10.cloned.1.call-done = bf16[4096,1024]{1,0:T(8,128)(2,1)} async-done(((bf16[256,1024]{1,0:T(8,128)(2,1)}), bf16[4096,1024]{1,0:T(8,128)(2,1)}) %all-gather.10.cloned.1.call-update) | async-done | bytes 8388624 | tf_op jit(solution)/shard_map/all_gather | solution.py:29
  411.8 10.1 %convolution_convert_fusion = bf16[512,1024]{1,0:T(8,128)(2,1)} fusion(bf16[512,4096]{0,1:T(8,128)(2,1)} %all-gather.6.cloned.1.call-done, bf16[4096,1024]{1,0:T(8,128)(2,1)} %all-gather.10.cloned.1.call-done), kind=kOutput, calls=%fused_computation.3 | convolution fusion | flops 4295491584 | bytes 13631488 | tf_op jit(solution)/shard_map/dot_general | solution.py:27
  422.9 64.1 %all-gather.12.cloned.1.call-done = bf16[1024,1024]{1,0:T(8,128)(2,1)} async-done(((bf16[512,1024]{1,0:T(8,128)(2,1)}), bf16[1024,1024]{1,0:T(8,128)(2,1)}) %all-gather.12.cloned.1.call-update) | async-done | bytes 2097168 | tf_op jit(solution)/shard_map/all_gather | solution.py:101
  487.0 2.2 reduce_sum.22
  489.2 1.2 fusion.1
  (41 shorter events, 3.5 us)
Async XLA Ops:
  11.8 23.5 %all-to-all-start = ((bf16[128,1,2]{2,1,0:T(2,128)(2,1)}), bf16[128,1,2]{2,1,0:T(2,128)(2,1)S(1)}, u32[]{:S(2)}, u32[]{:S(2)}) async-start(bf16[128,1,2]{2,1,0:T(2,128)(2,1)} %all_to_all.12), calls=%async_computation | async-start | bytes 131072 | tf_op jit(solution)/shard_map/all_to_all | solution.py:58
  31.6 12.1 %copy-start.2 = (s32[8,16]{1,0:T(8,128)S(1)}, s32[8,16]{1,0:T(8,128)}, u32[]{:S(2)}) copy-start(s32[8,16]{1,0:T(8,128)} %param.9) | copy-start | bytes 1540
  35.3 60.2 %all-to-all-start.1 = ((bf16[128,2,4096]{2,1,0:T(2,128)(2,1)}), bf16[128,2,4096]{2,1,0:T(2,128)(2,1)S(1)}, u32[]{:S(2)}, u32[]{:S(2)}) async-start(bf16[128,2,4096]{2,1,0:T(2,128)(2,1)} %reshape.102), calls=%async_computation.1 | async-start | bytes 4194304 | tf_op jit(solution)/shard_map/all_to_all | solution.py:51
  43.5 118.8 %all-gather.6.cloned.1.call-start = ((), (), s32[]{:S(2)}) async-start(), calls=%async_computation.2 | async-start | bytes 4718592 | tf_op jit(solution)/shard_map/all_gather | solution.py:95
  110.2 2.6 copy-start.1
  113.8 134.4 %all-gather.8.cloned.1.call-start = ((), (), s32[]{:S(2)}) async-start(), calls=%async_computation.3 | async-start | bytes 8912896 | tf_op jit(solution)/shard_map/all_gather | solution.py:29
  123.8 213.3 %all-reduce.2.cloned.1.call-start = ((), (), s32[]{:S(2)}) async-start(), calls=%async_computation.4 | async-start | bytes 2097152 | tf_op jit(solution)/shard_map/psum | solution.py:97
  258.4 153.4 %all-gather.10.cloned.1.call-start = ((), (), s32[]{:S(2)}) async-start(), calls=%async_computation.5 | async-start | bytes 8912896 | tf_op jit(solution)/shard_map/all_gather | solution.py:29
  339.0 82.9 %copy-start.3 = (s32[8,16]{1,0:T(8,128)S(1)}, s32[8,16]{1,0:T(8,128)}, u32[]{:S(2)}) copy-start(s32[8,16]{1,0:T(8,128)} %param.10) | copy-start | bytes 1540
  339.0 148.0 %all-gather.12.cloned.1.call-start = ((), (), s32[]{:S(2)}) async-start(), calls=%async_computation.6 | async-start | bytes 3145728 | tf_op jit(solution)/shard_map/all_gather | solution.py:101
  422.9 66.2 %copy-start = (bf16[512,1024]{1,0:T(8,128)(2,1)S(1)}, bf16[512,1024]{1,0:T(8,128)(2,1)}, u32[]{:S(2)}) copy-start(bf16[512,1024]{1,0:T(8,128)(2,1)} %all-reduce.2.cloned.1.call-done) | copy-start | bytes 3145732
Sparse Core Ops, SparseCore 0:
  114.0 48.3 all-gather.5
  164.7 83.4 all-gather.7
  258.5 78.5 all-reduce.1
  339.7 72.0 all-gather.9
  422.1 64.8 all-gather.11
